TPU v7x, 512 devices: a whole 4x8x8 slice. The times are simulated.
512 devices in a mesh: gx: 8 (over z), gy: 8 (over x, y_lo), gz: 8 (over y_hi, core).
Axes of the slice: x: 4, y: 8 (y_hi: 4, y_lo: 2; y = y_hi * 2 + y_lo), z: 8, core: 2. Of those that a mesh axis runs over, the one named last changes fastest.
Arguments:
- inputs: bfloat16 [512, 12288], P(('gx', 'gy'), 'gz'), may hold values from -6 to 6
- out_grad: bfloat16 [512, 12288], P(('gx', 'gy'), 'gz'), may hold values from -6 to 6
- preact: bfloat16 [512, 24576], P('gz', ('gx', 'gy')), may hold values from -6 to 6
- w_in: bfloat16 [12288, 24576], P('gz', ('gx', 'gy')), may hold values from -0.0546875 to 0.0546875
- w_out: bfloat16 [24576, 12288], P(('gx', 'gy'), 'gz'), may hold values from -0.0390625 to 0.0390625
Outputs:
- grad_input: bfloat16 [512, 12288], P(('gx', 'gy'), 'gz')
- grad_w_in: bfloat16 [12288, 24576], P('gz', ('gx', 'gy'))
- grad_w_out: bfloat16 [24576, 12288], P(('gx', 'gy'), 'gz')
All inputs are finite; a program needn't handle non-finite values.
Results may differ from a plain program's by a relative error of at most 0.0049.
Values may be sent and summed in bfloat16 or wider, within the bound.
No kernel may reach another device: no remote copies, remote signals or barrier semaphores. Data moves between devices by JAX's collectives and lax.ppermute only.
A program may use at most 64 MiB of HBM per device.

v0:
```python
import jax
import jax.numpy as jnp
from jax import lax
from jax.sharding import PartitionSpec as P

gelu_scale = 0.7978845608028654
cubic_coef = 0.044715


def gelu_parts(pre_float):
    tanh_arg = gelu_scale * (pre_float + cubic_coef * pre_float * pre_float * pre_float)
    tangent = jnp.tanh(tanh_arg)
    value = 0.5 * pre_float * (1.0 + tangent)
    slope = 0.5 * (1.0 + tangent) + 0.5 * pre_float * (1.0 - tangent * tangent) * gelu_scale * (
        1.0 + 3.0 * cubic_coef * pre_float * pre_float
    )
    return (value, slope)


def contract_rows(left, right):
    return lax.dot_general(
        left, right, (((1,), (1,)), ((), ())), preferred_element_type=jnp.float32
    )


def contract_cols(left, right):
    return lax.dot_general(
        left, right, (((0,), (0,)), ((), ())), preferred_element_type=jnp.float32
    )


def on_device(inputs, out_grad, preact, w_in, w_out):
    rows_x, rows_dy = (
        lax.all_gather(inputs, ("gx", "gy"), axis=0, tiled=True),
        lax.all_gather(out_grad, ("gx", "gy"), axis=0, tiled=True),
    )
    picked = rows_dy
    grad_hidden = lax.psum_scatter(
        contract_rows(picked, w_out), "gz", scatter_dimension=0, tiled=True
    )
    value_local, slope_local = gelu_parts(preact.astype(jnp.float32))
    grad_pre = (grad_hidden * slope_local).astype(jnp.bfloat16)
    hidden_local = value_local.astype(jnp.bfloat16)
    grad_all, hidden_all = (
        lax.all_gather(grad_pre, "gz", axis=0, tiled=True),
        lax.all_gather(hidden_local, "gz", axis=0, tiled=True),
    )
    grad_w_out = contract_cols(hidden_all, rows_dy).astype(jnp.bfloat16)
    grad_w_in = contract_cols(rows_x, grad_all).astype(jnp.bfloat16)
    picked = grad_all
    grad_input = lax.psum_scatter(
        contract_rows(picked, w_in), ("gx", "gy"), scatter_dimension=0, tiled=True
    ).astype(jnp.bfloat16)
    return (grad_input, grad_w_in, grad_w_out)


def solution(mesh):
    in_specs = (
        P(("gx", "gy"), "gz"),
        P(("gx", "gy"), "gz"),
        P("gz", ("gx", "gy")),
        P("gz", ("gx", "gy")),
        P(("gx", "gy"), "gz"),
    )
    out_specs = (P(("gx", "gy"), "gz"), P("gz", ("gx", "gy")), P(("gx", "gy"), "gz"))
    return jax.shard_map(
        on_device, mesh=mesh, in_specs=in_specs, out_specs=out_specs, check_vma=False
    )
```

profile of v0, /device:TPU:16, one launch (start us, length us, event | category | flops | bytes accessed | tf_op | source)
XLA Modules:
  0.0 995.1 jit_solution(596862571673999329)
XLA Ops:
  7.2 0.0 copy-start
  7.2 0.0 all-gather.3.cloned.1.call-start
  7.2 0.7 all-gather.3.cloned.1.call-update
  7.9 0.0 reduce-scatter.3.cloned.1.call-start
  8.0 309.0 %all-gather.3.cloned.1.call-done = bf16[512,1536]{1,0:T(8,128)(2,1)} async-done(((bf16[8,1536]{1,0:T(8,128)(2,1)}), bf16[512,1536]{1,0:T(8,128)(2,1)}) %all-gather.3.cloned.1.call-update) | async-done | bytes 1572880 | tf_op jit(solution)/shard_map/all_gather | solution.py:35
  317.0 3.6 fusion.12
  320.6 0.0 reduce-scatter.3.cloned.1.call-update
  320.6 0.0 all-gather.5.cloned.1.call-start
  320.7 0.7 all-gather.5.cloned.1.call-update
  321.4 0.0 reduce-scatter.5.cloned.1.call-start
  321.4 32.7 %reduce-scatter.3.cloned.1.call-done = f32[64,384]{1,0:T(8,128)} async-done(((f32[512,384]{1,0:T(8,128)}), f32[64,384]{1,0:T(8,128)}) %reduce-scatter.3.cloned.1.call-update) | async-done | bytes 98320 | tf_op jit(solution)/shard_map/reduce_scatter | solution.py:38
  354.1 0.0 copy-done.1
  354.1 1.0 fusion.8
  355.1 16.7 %all_gather.13 = bf16[512,384]{1,0:T(8,128)(2,1)S(1)} all-gather(bf16[64,384]{1,0:T(8,128)(2,1)S(1)} %get-tuple-element.7), channel_id=1, replica_groups=mesh['gx'=8,'gy'=8,'gz'=8] {'gz'}, dimensions={0}, use_global_device_ids=true | all-gather | bytes 442368 | tf_op jit(solution)/shard_map/all_gather | solution.py:45
  371.7 0.0 copy-done
  371.8 2.6 fusion.13
  374.4 0.0 reduce-scatter.5.cloned.1.call-update
  374.4 287.2 %all-gather.5.cloned.1.call-done = bf16[512,1536]{1,0:T(8,128)(2,1)} async-done(((bf16[8,1536]{1,0:T(8,128)(2,1)}), bf16[512,1536]{1,0:T(8,128)(2,1)}) %all-gather.5.cloned.1.call-update) | async-done | bytes 1572880 | tf_op jit(solution)/shard_map/all_gather | solution.py:34
  661.6 2.2 fusion
  663.8 1.4 copy.8
  665.2 15.2 %all_gather.15 = bf16[512,384]{1,0:T(8,128)(2,1)S(1)} all-gather(bf16[64,384]{1,0:T(8,128)(2,1)S(1)} %get-tuple-element.6), channel_id=1, replica_groups=mesh['gx'=8,'gy'=8,'gz'=8] {'gz'}, dimensions={0}, use_global_device_ids=true | all-gather | bytes 442368 | tf_op jit(solution)/shard_map/all_gather | solution.py:46
  680.4 3.2 convolution_convert_fusion
  683.6 303.5 %reduce-scatter.5.cloned.1.call-done = f32[8,1536]{1,0:T(8,128)} async-done(((f32[512,1536]{1,0:T(8,128)}), f32[8,1536]{1,0:T(8,128)}) %reduce-scatter.5.cloned.1.call-update) | async-done | bytes 49168 | tf_op jit(solution)/shard_map/reduce_scatter | solution.py:51
  987.2 1.4 convert_element_type.23
  (1 shorter events, 0.0 us)
Async XLA Ops:
  7.2 364.6 %copy-start = (bf16[1536,384]{1,0:T(8,128)(2,1)S(1)}, bf16[1536,384]{1,0:T(8,128)(2,1)}, u32[]{:S(2)}) copy-start(bf16[1536,384]{1,0:T(8,128)(2,1)} %param.8) | copy-start | bytes 3538948
  7.2 309.8 %all-gather.3.cloned.1.call-start = ((), (), s32[]{:S(2)}) async-start(), calls=%async_computation.2 | async-start | bytes 1597440 | tf_op jit(solution)/shard_map/all_gather | solution.py:35
  7.9 346.2 %copy-start.1 = (bf16[64,384]{1,0:T(8,128)(2,1)S(1)}, bf16[64,384]{1,0:T(8,128)(2,1)}, u32[]{:S(2)}) copy-start(bf16[64,384]{1,0:T(8,128)(2,1)} %param.7) | copy-start | bytes 147460
  7.9 346.2 %reduce-scatter.3.cloned.1.call-start = ((), (), s32[]{:S(2)}) async-start(), calls=%async_computation.3 | async-start | bytes 884736 | tf_op jit(solution)/shard_map/reduce_scatter | solution.py:38
  320.6 341.0 %all-gather.5.cloned.1.call-start = ((), (), s32[]{:S(2)}) async-start(), calls=%async_computation.5 | async-start | bytes 1597440 | tf_op jit(solution)/shard_map/all_gather | solution.py:34
  321.4 665.8 %reduce-scatter.5.cloned.1.call-start = ((), (), s32[]{:S(2)}) async-start(), calls=%async_computation.4 | async-start | bytes 3194880 | tf_op jit(solution)/shard_map/reduce_scatter | solution.py:51
Sparse Core Ops, SparseCore 0:
  10.1 306.8 all-gather.2
  320.8 33.3 reduce-scatter.2
  356.4 305.1 all-gather.4
  664.5 322.6 reduce-scatter.4
where the time goes:
time: 995 us
  waiting for transfers between devices  934 us (94%)
  blocking collectives  31.8 us (3%)
  between operations  13.8 us (1%)
  matrix products  11.7 us (1%)
    all_gather x1, waiting for transfers between devices, on_device(): lax.all_gather(out_grad, ('gx', 'gy'), axis=0, tiled=True)  309 us
    reduce_scatter x1, waiting for transfers between devices, on_device(): lax.psum_scatter(contract_rows(picked, w_in), ('gx', 'gy'), scatter_dimen...  304 us
    all_gather x1, waiting for transfers between devices, on_device(): lax.all_gather(inputs, ('gx', 'gy'), axis=0, tiled=True)  287 us
    reduce_scatter x1, waiting for transfers between devices, on_device(): lax.psum_scatter(contract_rows(picked, w_out), 'gz', scatter_dimension=0,...  32.7 us
  transfers between devices with their start and end apart: 4, of which 4 were waited for; matrix products, arithmetic and copies ran while one was open for 1% of the time, Pallas kernels for 0%

commit v1 on v0

--- a/solution.py
+++ b/solution.py
@@ -31,7 +31,10 @@
 
 def on_device(inputs, out_grad, preact, w_in, w_out):
     rows_x, rows_dy = (
-        lax.all_gather(inputs, ("gx", "gy"), axis=0, tiled=True),
+        jnp.concatenate(
+            lax.all_to_all(jnp.stack([inputs] * lax.axis_size(("gx", "gy"))), ("gx", "gy"), 0, 0),
+            axis=0,
+        ),
         lax.all_gather(out_grad, ("gx", "gy"), axis=0, tiled=True),
     )
     picked = rows_dy

time: 995 us -> 712 us (0.72)
  waiting for transfers between devices: 934 us -> 598 us
  blocking collectives: 31.8 us -> 85.4 us
    all_gather x1 -> x0, waiting for transfers between devices: 287 us -> none  [on_device(): lax.all_gather(inputs, ('gx', 'gy'), axis=0, tiled=True)]
    all_to_all x0 -> x1, blocking collectives: none -> 53.5 us  [on_device(): lax.all_to_all(jnp.stack([inputs] * lax.axis_size(('gx', 'gy'))), ('gx',...]
    reduce_scatter x1, waiting for transfers between devices: 304 us -> 255 us  [on_device(): lax.psum_scatter(contract_rows(picked, w_in), ('gx', 'gy'), scatter_dimen...]
  transfers between devices with their start and end apart: 4 -> 3, of which waited for: 4 -> 3; matrix products, arithmetic and copies ran while one was open for 1% -> 1% of each run, Pallas kernels for 0% -> 0%
where the time goes in v1:
time: 712 us
  waiting for transfers between devices  598 us (84%)
  blocking collectives  85.4 us (12%)
  between operations  13.8 us (2%)
  matrix products  10.3 us (1%)
    all_gather x1, waiting for transfers between devices, on_device(): lax.all_gather(out_grad, ('gx', 'gy'), axis=0, tiled=True)  309 us
    reduce_scatter x1, waiting for transfers between devices, on_device(): lax.psum_scatter(contract_rows(picked, w_in), ('gx', 'gy'), scatter_dimen...  255 us
    all_to_all x1, blocking collectives, on_device(): lax.all_to_all(jnp.stack([inputs] * lax.axis_size(('gx', 'gy'))), ('gx',...  53.5 us
    reduce_scatter x1, waiting for transfers between devices, on_device(): lax.psum_scatter(contract_rows(picked, w_out), 'gz', scatter_dimension=0,...  33.4 us
    all_gather x1, blocking collectives, on_device(): lax.all_gather(grad_pre, 'gz', axis=0, tiled=True)  16.7 us
    all_gather x1, blocking collectives, on_device(): lax.all_gather(hidden_local, 'gz', axis=0, tiled=True)  15.3 us
  transfers between devices with their start and end apart: 3, of which 3 were waited for; matrix products, arithmetic and copies ran while one was open for 1% of the time, Pallas kernels for 0%

profile of v1, /device:TPU:16, one launch (start us, length us, event | category | flops | bytes accessed | tf_op | source)
XLA Modules:
  0.0 712.1 jit_solution(5221708911343416166)
XLA Ops:
  7.2 0.0 copy-start
  7.2 0.0 all-gather.2.cloned.1.call-start
  7.2 0.7 all-gather.2.cloned.1.call-update
  7.9 0.0 reduce-scatter.3.cloned.1.call-start
  8.0 309.0 %all-gather.2.cloned.1.call-done = bf16[512,1536]{1,0:T(8,128)(2,1)} async-done(((bf16[8,1536]{1,0:T(8,128)(2,1)}), bf16[512,1536]{1,0:T(8,128)(2,1)}) %all-gather.2.cloned.1.call-update) | async-done | bytes 1572880 | tf_op jit(solution)/shard_map/all_gather | solution.py:38
  317.0 3.6 fusion.13
  320.6 0.0 reduce-scatter.3.cloned.1.call-update
  320.6 0.0 reduce-scatter.5.cloned.1.call-start
  320.7 33.4 %reduce-scatter.3.cloned.1.call-done = f32[64,384]{1,0:T(8,128)} async-done(((f32[512,384]{1,0:T(8,128)}), f32[64,384]{1,0:T(8,128)}) %reduce-scatter.3.cloned.1.call-update) | async-done | bytes 98320 | tf_op jit(solution)/shard_map/reduce_scatter | solution.py:41
  354.1 0.0 copy-done.1
  354.1 1.0 fusion.9
  355.1 16.7 %all_gather.10 = bf16[512,384]{1,0:T(8,128)(2,1)S(1)} all-gather(bf16[64,384]{1,0:T(8,128)(2,1)S(1)} %get-tuple-element.7), channel_id=1, replica_groups=mesh['gx'=8,'gy'=8,'gz'=8] {'gz'}, dimensions={0}, use_global_device_ids=true | all-gather | bytes 442368 | tf_op jit(solution)/shard_map/all_gather | solution.py:48
  371.7 0.0 copy-done
  371.8 2.7 fusion.14
  374.4 0.0 reduce-scatter.5.cloned.1.call-update
  374.4 0.7 copy-done.2
  375.1 0.1 stack.2
  375.3 53.5 %all_to_all.5 = bf16[64,8,1536]{2,1,0:T(8,128)(2,1)S(1)} all-to-all(bf16[64,8,1536]{2,1,0:T(8,128)(2,1)S(1)} %stack.2), channel_id=1, replica_groups=mesh['gx'=8,'gy'=8,'gz'=8] {'gx','gy'}, dimensions={0} | all-to-all | bytes 3145728 | tf_op jit(solution)/shard_map/all_to_all | solution.py:35
  428.7 0.8 fusion
  429.5 1.4 copy.8
  430.9 15.3 %all_gather.11 = bf16[512,384]{1,0:T(8,128)(2,1)S(1)} all-gather(bf16[64,384]{1,0:T(8,128)(2,1)S(1)} %get-tuple-element.6), channel_id=1, replica_groups=mesh['gx'=8,'gy'=8,'gz'=8] {'gz'}, dimensions={0}, use_global_device_ids=true | all-gather | bytes 442368 | tf_op jit(solution)/shard_map/all_gather | solution.py:49
  446.2 3.2 convolution_convert_fusion
  449.4 254.7 %reduce-scatter.5.cloned.1.call-done = f32[8,1536]{1,0:T(8,128)} async-done(((f32[512,1536]{1,0:T(8,128)}), f32[8,1536]{1,0:T(8,128)}) %reduce-scatter.5.cloned.1.call-update) | async-done | bytes 49168 | tf_op jit(solution)/shard_map/reduce_scatter | solution.py:54
  704.2 1.4 convert_element_type.23
  (2 shorter events, 0.0 us)
Async XLA Ops:
  7.2 364.6 %copy-start = (bf16[1536,384]{1,0:T(8,128)(2,1)S(1)}, bf16[1536,384]{1,0:T(8,128)(2,1)}, u32[]{:S(2)}) copy-start(bf16[1536,384]{1,0:T(8,128)(2,1)} %param.8) | copy-start | bytes 3538948
  7.2 309.8 %all-gather.2.cloned.1.call-start = ((), (), s32[]{:S(2)}) async-start(), calls=%async_computation.3 | async-start | bytes 1597440 | tf_op jit(solution)/shard_map/all_gather | solution.py:38
  7.9 346.2 %copy-start.1 = (bf16[64,384]{1,0:T(8,128)(2,1)S(1)}, bf16[64,384]{1,0:T(8,128)(2,1)}, u32[]{:S(2)}) copy-start(bf16[64,384]{1,0:T(8,128)(2,1)} %param.7) | copy-start | bytes 147460
  7.9 346.2 %reduce-scatter.3.cloned.1.call-start = ((), (), s32[]{:S(2)}) async-start(), calls=%async_computation.4 | async-start | bytes 884736 | tf_op jit(solution)/shard_map/reduce_scatter | solution.py:41
  320.6 383.5 %reduce-scatter.5.cloned.1.call-start = ((), (), s32[]{:S(2)}) async-start(), calls=%async_computation.5 | async-start | bytes 3194880 | tf_op jit(solution)/shard_map/reduce_scatter | solution.py:54
  374.4 0.7 copy-start.2
Sparse Core Ops, SparseCore 0:
  10.1 306.8 all-gather.1
  320.8 33.3 reduce-scatter.2
  374.6 329.5 reduce-scatter.4
